TPU v7x, 32 devices: a whole 2x2x4 slice. The times are simulated.
32 devices in a mesh: groups: 2 (over y), enrol: 4 (over z), probe: 4 (over x, core).
Axes of the slice: x: 2, y: 2, z: 4, core: 2. Of those that a mesh axis runs over, the one named last changes fastest.
Arguments:
- images: float32 [16384, 512], P(('groups', 'enrol', 'probe')), parts along dimension 0, may hold values from -6 to 6
- w_first: float32 [512, 2048], replicated, may hold values from -0.25 to 0.25
- w_second: float32 [2048, 256], replicated, may hold values from -0.125 to 0.125
- calib_scale: float32 [1], replicated, may hold values from 5 to 20
- calib_bias: float32 [1], replicated, may hold values from -2 to 2
- template_slot: int32 [16384], P(('groups', 'enrol', 'probe')), parts along dimension 0, may hold values from 0 to 191
- media_counts: int32 [32, 16], P(('groups', 'enrol', 'probe')), parts along dimension 0, may hold values from 1 to 64, as said below
Outputs:
- scores: bfloat16 [4096, 1024], P(('groups', 'enrol'), 'probe'), parts along dimension 0
There are 2 independent parts, one for each index of `groups`. A program takes and returns all parts, laid end to end along the dimension named above; an argument that names none is the same for every part. Nothing has to cross between parts.
Inputs may be any that keep to these rules, and one draw needn't show every extreme that they name: `media_counts`: each row sums to 512; in every draw one owner receives exactly 64 images from every device.
All inputs are finite; a program needn't handle non-finite values.
Results may differ from a plain program's by a relative error of at most 0.001.
Values sent between devices are 32-bit elements; how exact they have to be, the bound alone decides.
No kernel may reach another device: no remote copies, remote signals or barrier semaphores. Data moves between devices by JAX's collectives and lax.ppermute only.
A program may use at most 64 MiB of HBM per device.

v0:
```python
import functools
import math

import jax
import jax.numpy as jnp
from jax import lax
from jax.experimental import pallas as pl
from jax.experimental.pallas import tpu as pltpu
from jax.sharding import PartitionSpec as P


ET_OWN = 128
PT_OWN = 64
SLOTS = ET_OWN + PT_OWN
NONE = -4096
EPS = 1e-06
LANES = 128
CHUNK = 256
PIECE = 32
GROUP = 4
STARTS = (1, 1, 1, 2)
LATE = 6
F32 = jnp.float32
BF16 = jnp.bfloat16
ROOT = math.sqrt(2.0 / math.pi)


def split(value):
    high = value.astype(BF16)
    return high, (value - high.astype(F32)).astype(BF16)


def unit(table):
    return table * lax.rsqrt(jnp.sum(table * table, axis=-1, keepdims=True) + EPS)


def dot(a, b, dims=((1,), (0,))):
    return lax.dot_general(a, b, (dims, ((), ())), preferred_element_type=F32)


def place(n_enrol, n_probe):
    z, p = lax.axis_index("enrol"), lax.axis_index("probe")
    rows, chips = n_enrol // 2, n_probe // 2
    return z // rows, (z % rows) * chips + p // 2, p % 2


def twice_gelu(x):
    return x + x * jnp.tanh(x * (ROOT + (ROOT * 0.044715) * (x * x)))


def embed_kernel(n_enrol, n_probe, count_hbm, slots_hbm, images, w_first, w_second, *rest):
    chips = n_enrol * n_probe // 4
    owners = n_enrol * n_probe
    far, near = rest[:chips], rest[chips : 2 * chips]
    (img, w1, w2, x3, w3, pre, h3, v3, feature, emb, slots, table, count, ends, sem_img, sem_w1, sem_w2, sem_small) = rest[
        2 * chips :
    ]
    n_img, d_in = images.shape
    width = w_second.shape[1]
    pieces = w1.shape[0]
    block = near[0].shape[0]

    def copy_first(j):
        columns = w_first.at[:, pl.ds(pl.multiple_of(j * CHUNK, CHUNK), CHUNK)]
        return pltpu.make_async_copy(columns, w1.at[j], sem_w1.at[j])

    def copy_second(j):
        part = w_second.at[pl.ds(pl.multiple_of(j * CHUNK, CHUNK), CHUNK)]
        return pltpu.make_async_copy(part, w2.at[j], sem_w2.at[j])

    quarter = n_img // 4
    image_copies = [
        pltpu.make_async_copy(
            images.at[pl.ds(q * quarter, quarter)], img.at[pl.ds(q * quarter, quarter)], sem_img.at[q]
        )
        for q in range(4)
    ]
    for copy in image_copies:
        copy.start()
    copy_first(0).start()
    queue = [copy_first(1), copy_first(2), copy_second(0)]
    for j in range(3, pieces):
        queue += [copy_first(j), copy_second(j - 2)]
    queue += [copy_second(pieces - 2), copy_second(pieces - 1)]

    def start_more(n):
        for copy in queue[:n]:
            copy.start()
        del queue[:n]

    small = [
        pltpu.make_async_copy(count_hbm, count, sem_small.at[0]),
        pltpu.make_async_copy(slots_hbm, slots, sem_small.at[1]),
    ]
    for copy in small:
        copy.start()

    def thrice(source, target, rows):
        for r in range(0, rows, PIECE):
            high, low = split(source[pl.ds(r, PIECE), :])
            target[pl.ds(r, PIECE), :] = high
            target[pl.ds(rows + r, PIECE), :] = high
            target[pl.ds(2 * rows + r, PIECE), :] = low

    def first(s):
        pre[s] = dot(x3[...], w3[s])

    def load(j, s):
        thrice(w1.at[j], w3.at[s], d_in)

    def bend(s):
        for r in range(0, n_img, PIECE):
            at = pl.ds(r, PIECE)
            high, low = split(twice_gelu(pre[s, at, :]))
            h3[s, at, 0:CHUNK] = high
            h3[s, at, CHUNK : 2 * CHUNK] = low
            h3[s, at, 2 * CHUNK :] = high

    def second(j, s):
        thrice(w2.at[j], v3.at[s], CHUNK)
        feature[...] = feature[...] + dot(h3[s], v3[s])

    for q, copy in enumerate(image_copies):
        copy.wait()
        start_more(STARTS[q])
        for r in range(q * quarter, (q + 1) * quarter, PIECE):
            at = pl.ds(r, PIECE)
            high, low = split(img[at, :])
            x3[at, 0:d_in] = high
            x3[at, d_in : 2 * d_in] = low
            x3[at, 2 * d_in :] = high
    copy_first(0).wait()
    start_more(len(queue) - LATE)
    load(0, 0)
    first(0)
    copy_first(1).wait()
    start_more(len(queue))
    load(1, 1)
    feature[...] = jnp.zeros_like(feature)

    def trip(i, carry):
        @pl.when(i == 0)
        def _():
            for j in range(GROUP):
                copy_first(j + 2).wait()
                copy_second(j).wait()

        @pl.when(i == 1)
        def _():
            for j in range(GROUP, pieces):
                if j + 2 < pieces:
                    copy_first(j + 2).wait()
                copy_second(j).wait()

        for step in range(GROUP):
            j, s = GROUP * i + step, step % 2
            bend(s)
            first(1 - s)
            load(jnp.minimum(j + 2, pieces - 1), s)
            second(j, s)
        return carry

    lax.fori_loop(0, pieces // GROUP, trip, 0)

    for copy in small:
        copy.wait()
    ends[0] = 0
    rows = slots.shape[0]
    position = lax.broadcasted_iota(jnp.int32, (rows, LANES), 0) * LANES
    position = position + lax.broadcasted_iota(jnp.int32, (rows, LANES), 1)
    odd = jnp.zeros((rows, LANES), jnp.int32)
    total = jnp.int32(0)
    for o in range(owners):
        total = total + count[0, o]
        ends[o + 1] = total
        odd = jnp.where(position >= total, (o + 1) % 2, odd)
    table[...] = jnp.full(table.shape, NONE, jnp.int32)
    table[0:rows, :] = slots[...] + SLOTS * odd

    tiles = width // LANES
    for r in range(0, n_img, PIECE):
        rows = unit(0.5 * feature[pl.ds(r, PIECE), :])
        for t in range(tiles):
            emb[t, pl.ds(r, PIECE), :] = rows[:, t * LANES : (t + 1) * LANES]
    for t in range(tiles):
        emb[t, n_img : n_img + block, :] = jnp.zeros((block, LANES), F32)

    half, chip, _ = place(n_enrol, n_probe)
    lane = lax.broadcasted_iota(jnp.int32, (1, LANES), 1)

    def window(start, size):
        row, shift = start // LANES, start % LANES
        back = (LANES - shift) % LANES
        one = pltpu.roll(table[pl.ds(row, 1), :], back, 1)
        two = pltpu.roll(table[pl.ds(row + 1, 1), :], back, 1)
        ids = jnp.where(lane < LANES - shift, one, two)
        return jnp.where(lane < size, ids, NONE).astype(F32)

    for k in range(chips):
        to = chip ^ k
        for side in range(2):
            pair = (half if side else 1 - half) * chips + to
            start, stop = ends[2 * pair], ends[2 * pair + 2]
            out = near[k] if side else far[k]
            for t in range(tiles):
                out[0:block, t * LANES : (t + 1) * LANES] = emb[t, pl.ds(start, block), :]
            far[k][block + side : block + side + 1, 0:LANES] = window(start, stop - start)


def embed(n_enrol, n_probe, images, w_first, w_second, slots, count):
    chips = n_enrol * n_probe // 4
    n_img, d_in = images.shape
    width = w_second.shape[1]
    pieces = w_second.shape[0] // CHUNK
    block = 4 * n_img // (n_enrol * n_probe)
    vmem = pl.BlockSpec(memory_space=pltpu.VMEM)
    hbm = pl.BlockSpec(memory_space=pltpu.HBM)
    inputs = count, slots.reshape(n_img // LANES, LANES), images, w_first, w_second
    outs = pl.pallas_call(
        functools.partial(embed_kernel, n_enrol, n_probe),
        out_shape=[jax.ShapeDtypeStruct((block + 8, width), F32)] * chips
        + [jax.ShapeDtypeStruct((block, width), F32)] * chips,
        in_specs=[hbm] * 5,
        out_specs=[vmem] * (2 * chips),
        scratch_shapes=[
            pltpu.VMEM((n_img, d_in), F32),
            pltpu.VMEM((pieces, d_in, CHUNK), F32),
            pltpu.VMEM((pieces, CHUNK, width), F32),
            pltpu.VMEM((n_img, 3 * d_in), BF16),
            pltpu.VMEM((2, 3 * d_in, CHUNK), BF16),
            pltpu.VMEM((2, n_img, CHUNK), F32),
            pltpu.VMEM((2, n_img, 3 * CHUNK), BF16),
            pltpu.VMEM((2, 3 * CHUNK, width), BF16),
            pltpu.VMEM((n_img, width), F32),
            pltpu.VMEM((width // LANES, n_img + block, LANES), F32),
            pltpu.VMEM((n_img // LANES, LANES), jnp.int32),
            pltpu.VMEM((n_img // LANES + 8 - n_img // LANES % 8, LANES), jnp.int32),
            pltpu.SMEM((1, n_enrol * n_probe), jnp.int32),
            pltpu.SMEM((n_enrol * n_probe + 1,), jnp.int32),
            pltpu.SemaphoreType.DMA((4,)),
            pltpu.SemaphoreType.DMA((pieces,)),
            pltpu.SemaphoreType.DMA((pieces,)),
            pltpu.SemaphoreType.DMA((2,)),
        ],
        compiler_params=pltpu.CompilerParams(vmem_limit_bytes=52 << 20),
        name="embed",
    )(*[pltpu.with_memory_space_constraint(x, pltpu.HBM) for x in inputs])
    return outs[:chips], outs[chips:]


def picked(half, ids, side, rows):
    block = rows.shape[0] if side else rows.shape[0] - 8
    at = ids.shape[0] - 8 + side
    want = ids[at : at + 1, 0:LANES][:, :block].astype(jnp.int32)
    core = lax.axis_index("probe") % 2
    want = want - (core ^ half) * SLOTS
    slot = lax.broadcasted_iota(jnp.int32, (SLOTS, block), 0)
    pick = (slot == want).astype(F32).astype(BF16)
    high, low = split(rows[0:block, :])
    return dot(pick, high) + dot(pick, low)


def pool_own_kernel(side, ids, rows, mine, other):
    mine[...] = picked(0, ids, side, rows)
    other[...] = picked(1, ids, side, rows)


def pool_one_kernel(half, ids, rows, out):
    out[...] = picked(half, ids, 1, rows)


def pool_kernel(side, half, count, *refs):
    ids, rows = refs[:count], refs[count : 2 * count] if side else refs[:count]
    before, out = refs[-2:]
    sums = before[...]
    for k in range(count):
        sums = sums + picked(half, ids[k], side, rows[k])
    out[...] = sums


def local(kernel, outs, *args, limit=8 << 20, kind=F32):
    vmem = pl.BlockSpec(memory_space=pltpu.VMEM)
    return pl.pallas_call(
        kernel,
        out_shape=[jax.ShapeDtypeStruct(shape, kind) for shape in outs],
        in_specs=[vmem] * len(args),
        out_specs=[vmem] * len(outs),
        compiler_params=pltpu.CompilerParams(vmem_limit_bytes=limit),
    )(*args)


def add_kernel(a, b, out):
    out[...] = a[...] + b[...]


def prepare_kernel(own, other, own_out, other_out):
    width = own.shape[1]
    for table, out in ((own, own_out), (other, other_out)):
        out[:, :width], out[:, width:] = split(unit(table[...]))


def score_kernel(n_enrol, n_probe, scale, bias, *refs):
    rows, cols = n_enrol // 2, n_probe // 2
    enrol, probe = refs[: 2 * cols], refs[2 * cols : 2 * cols + 2 * rows]
    out, e3, p3 = refs[2 * cols + 2 * rows :]
    width = probe[0].shape[1]
    z, p = lax.axis_index("enrol"), lax.axis_index("probe")

    def put(table, start, size, high_low):
        at = pl.ds(pl.multiple_of(start * size, size), size)
        for t, part in enumerate(high_low):
            table[at, t * width : (t + 1) * width] = part

    for k in range(rows):
        for side in range(2):
            high, low = split(unit(probe[2 * k + side][...]))
            put(p3, z ^ k ^ (side * rows), PT_OWN, (high, high, low))
    for k in range(n_probe):
        if k < 2:
            high, low = enrol[k][:, :width], enrol[k][:, width:]
        else:
            high, low = split(unit(enrol[k][...]))
        put(e3, p ^ k, ET_OWN, (high, low, high))
    cosine = dot(e3[...], p3[...], ((1,), (1,)))
    out[...] = jax.nn.sigmoid(scale[0] * cosine + bias[0]).astype(BF16)


def score(n_enrol, n_probe, scale, bias, enrol, probe):
    width = probe[0].shape[1]
    vmem = pl.BlockSpec(memory_space=pltpu.VMEM)
    smem = pl.BlockSpec(memory_space=pltpu.SMEM)
    return pl.pallas_call(
        functools.partial(score_kernel, n_enrol, n_probe),
        out_shape=jax.ShapeDtypeStruct((n_probe * ET_OWN, n_enrol * PT_OWN), BF16),
        in_specs=[smem, smem] + [vmem] * (len(enrol) + len(probe)),
        out_specs=vmem,
        scratch_shapes=[
            pltpu.VMEM((n_probe * ET_OWN, 3 * width), BF16),
            pltpu.VMEM((n_enrol * PT_OWN, 3 * width), BF16),
        ],
        compiler_params=pltpu.CompilerParams(vmem_limit_bytes=8 << 20),
        name="score",
    )(scale, bias, *enrol, *probe)


def solution(mesh):
    n_enrol, n_probe = mesh.shape["enrol"], mesh.shape["probe"]
    rows, cols = n_enrol // 2, n_probe // 2
    chips = rows * cols

    def flip(value, enrol_bits, probe_bits):
        pairs = [
            (z * n_probe + p, (z ^ enrol_bits) * n_probe + (p ^ probe_bits))
            for z in range(n_enrol)
            for p in range(n_probe)
        ]
        return lax.ppermute(value, ("enrol", "probe"), pairs)

    def across_chips(blocks):
        moved = []
        for k in range(1, chips):
            moved.append(flip(blocks[k], k // cols, 2 * (k % cols)))
        return moved

    def body(images, w_first, w_second, scale, bias, template_slot, media_counts):
        far, near = embed(n_enrol, n_probe, images, w_first, w_second, template_slot, media_counts)
        sums = (SLOTS, w_second.shape[1])
        far_in = across_chips(far)
        near_in = across_chips(near)
        kernel = functools.partial(pool_own_kernel, 0)
        far_mine, far_other = local(kernel, [sums] * 2, far[0], far[0])
        kernel = functools.partial(pool_one_kernel, 0)
        (near_mine,) = local(kernel, [sums], far[0], near[0])
        kernel = functools.partial(pool_one_kernel, 1)
        (near_other,) = local(kernel, [sums], far[0], near[0])

        def pool(side, half, *args):
            kernel = functools.partial(pool_kernel, side, half, chips - 1)
            return local(kernel, [sums], *args)[0]

        far_other = pool(0, 1, *far_in, far_other)
        far_other = flip(far_other, 0, 1)
        far_mine = pool(0, 0, *far_in, far_mine)
        far_enrol, far_probe = lax.optimization_barrier(
            (far_mine[:ET_OWN] + far_other[:ET_OWN], far_mine[ET_OWN:] + far_other[ET_OWN:])
        )
        enrol_far = flip(far_enrol, rows, 0)
        own_far = flip(far_probe, rows, 0)
        near_other = pool(1, 1, *far_in, *near_in, near_other)
        near_mine = pool(1, 0, *far_in, *near_in, near_mine)
        near_other = flip(near_other, 0, 1)
        near_probe = near_mine[ET_OWN:] + near_other[ET_OWN:]
        probe_far = flip(near_probe, rows, 0)
        (near_sum,) = local(add_kernel, [sums], near_mine, near_other)
        enrol = near_sum[:ET_OWN] + enrol_far
        own_probe = near_sum[ET_OWN:] + own_far
        across_probe = far_probe + probe_far
        probe_parts = []
        for k in range(rows):
            for part in (own_probe, across_probe):
                probe_parts.append(flip(part, k, 0) if k else part)
        pair = (ET_OWN, 2 * enrol.shape[1])
        enrol_parts = [enrol, flip(enrol, 0, 1)]
        enrol_parts = [*local(prepare_kernel, [pair] * 2, *enrol_parts, kind=BF16)]
        for k in range(1, cols):
            part = flip(enrol, 0, 2 * k)
            enrol_parts += [part, flip(part, 0, 1)]
        return score(n_enrol, n_probe, scale, bias, enrol_parts, probe_parts)

    return jax.shard_map(
        body,
        mesh=mesh,
        in_specs=(
            P(("groups", "enrol", "probe"), None),
            P(),
            P(),
            P(),
            P(),
            P(("groups", "enrol", "probe")),
            P(("groups", "enrol", "probe"), None),
        ),
        out_specs=P(("groups", "enrol"), "probe"),
        check_vma=False,
    )
```

profile of v0, /device:TPU:0, one launch (start us, length us, event | category | flops | bytes accessed | tf_op | source)
XLA Modules:
  0.0 55.7 jit_solution(2918499150965633144)
XLA Ops:
  0.0 8.7 %embed.1 = (f32[136,256]{1,0:T(8,128)S(1)}, f32[136,256]{1,0:T(8,128)S(1)}, f32[136,256]{1,0:T(8,128)S(1)}, f32[136,256]{1,0:T(8,128)S(1)}, f32[128,256]{1,0:T(8...) custom-call(s32[1,16]{1,0:T(1,128)} %count_hbm.1, s32[4,128]{1,0:T(4,128)} %bitcast.1, ...), custom_call_target="tpu_custom_call" | custom-call | tf_op jit(solution)/shard_map/embed/pallas_call | solution.py:219
  8.7 3.0 %collective-permute-start = (f32[136,256]{1,0:T(8,128)S(1)}, f32[136,256]{1,0:T(8,128)S(1)}, u32[]{:S(2)}, u32[]{:S(2)}) collective-permute-start(f32[136,256]{1,0:T(8,128)S(1)} %get-tuple-element.19), channel_id=1, source_target_pairs={{0,2},{1,3},{2,0},{3,1},{4,6},{5,7},{6,4},{7,5},{8,10},{9,11},{10,... | collective-permute-start | bytes 417800 | tf_op jit(solution)/shard_map/ppermute | solution.py:357
  11.8 1.6 %collective-permute-start.1 = (f32[136,256]{1,0:T(8,128)S(1)}, f32[136,256]{1,0:T(8,128)S(1)}, u32[]{:S(2)}, u32[]{:S(2)}) collective-permute-start(f32[136,256]{1,0:T(8,128)S(1)} %get-tuple-element.20), channel_id=1, source_target_pairs={{0,4},{1,5},{2,6},{3,7},{4,0},{5,1},{6,2},{7,3},{8,12},{9,13},{10,... | collective-permute-start | bytes 417800 | tf_op jit(solution)/shard_map/ppermute | solution.py:357
  13.4 0.2 shard_map.78
  13.6 1.8 %collective-permute-done.refs_0_ = f32[136,256]{1,0:T(8,128)S(1)} collective-permute-done((f32[136,256]{1,0:T(8,128)S(1)}, f32[136,256]{1,0:T(8,128)S(1)}, u32[]{:S(2)}, u32[]{:S(2)}) %collective-permute-start) | collective-permute-done | bytes 139296 | tf_op jit(solution)/shard_map/ppermute | solution.py:357
  15.4 2.9 %collective-permute-done.1.refs_1_ = f32[136,256]{1,0:T(8,128)S(1)} collective-permute-done((f32[136,256]{1,0:T(8,128)S(1)}, f32[136,256]{1,0:T(8,128)S(1)}, u32[]{:S(2)}, u32[]{:S(2)}) %collective-permute-start.1) | collective-permute-done | bytes 139296 | tf_op jit(solution)/shard_map/ppermute | solution.py:357
  18.3 1.4 %collective-permute-done.2.refs_2_ = f32[136,256]{1,0:T(8,128)S(1)} collective-permute-done((f32[136,256]{1,0:T(8,128)S(1)}, f32[136,256]{1,0:T(8,128)S(1)}, u32[]{:S(2)}, u32[]{:S(2)}) %collective-permute-start.2) | collective-permute-done | bytes 139296 | tf_op jit(solution)/shard_map/ppermute | solution.py:357
  19.7 0.3 shard_map.80
  20.1 1.7 %collective-permute-start.3 = (f32[128,256]{1,0:T(8,128)S(1)}, f32[128,256]{1,0:T(8,128)S(1)}, u32[]{:S(2)}, u32[]{:S(2)}) collective-permute-start(f32[128,256]{1,0:T(8,128)S(1)} %get-tuple-element.22), channel_id=1, source_target_pairs={{0,2},{1,3},{2,0},{3,1},{4,6},{5,7},{6,4},{7,5},{8,10},{9,11},{10,... | collective-permute-start | bytes 393224 | tf_op jit(solution)/shard_map/ppermute | solution.py:357
  21.8 1.6 %collective-permute-start.4 = (f32[128,256]{1,0:T(8,128)S(1)}, f32[128,256]{1,0:T(8,128)S(1)}, u32[]{:S(2)}, u32[]{:S(2)}) collective-permute-start(f32[128,256]{1,0:T(8,128)S(1)} %get-tuple-element.23), channel_id=1, source_target_pairs={{0,4},{1,5},{2,6},{3,7},{4,0},{5,1},{6,2},{7,3},{8,12},{9,13},{10,... | collective-permute-start | bytes 393224 | tf_op jit(solution)/shard_map/ppermute | solution.py:357
  23.4 0.3 collective-permute-start.5
  23.7 0.2 shard_map.75.refs_6_
  23.9 2.1 %collective-permute-done.3.refs_3_ = f32[128,256]{1,0:T(8,128)S(1)} collective-permute-done((f32[128,256]{1,0:T(8,128)S(1)}, f32[128,256]{1,0:T(8,128)S(1)}, u32[]{:S(2)}, u32[]{:S(2)}) %collective-permute-start.3) | collective-permute-done | bytes 131104 | tf_op jit(solution)/shard_map/ppermute | solution.py:357
  26.0 2.2 %collective-permute-done.4.refs_4_ = f32[128,256]{1,0:T(8,128)S(1)} collective-permute-done((f32[128,256]{1,0:T(8,128)S(1)}, f32[128,256]{1,0:T(8,128)S(1)}, u32[]{:S(2)}, u32[]{:S(2)}) %collective-permute-start.4) | collective-permute-done | bytes 131104 | tf_op jit(solution)/shard_map/ppermute | solution.py:357
  28.2 1.8 %collective-permute-done.5.refs_5_ = f32[128,256]{1,0:T(8,128)S(1)} collective-permute-done((f32[128,256]{1,0:T(8,128)S(1)}, f32[128,256]{1,0:T(8,128)S(1)}, u32[]{:S(2)}, u32[]{:S(2)}) %collective-permute-start.5) | collective-permute-done | bytes 131104 | tf_op jit(solution)/shard_map/ppermute | solution.py:357
  30.0 0.3 shard_map.76
  30.4 0.3 shard_map.79
  30.8 2.8 %collective-permute-start.8 = (f32[128,256]{1,0:T(8,128)S(1)}, f32[128,256]{1,0:T(8,128)S(1)}, u32[]{:S(2)}, u32[]{:S(2)}) collective-permute-start(f32[128,256]{1,0:T(8,128)S(1)} %slice_add_fusion), channel_id=1, source_target_pairs={{0,8},{1,9},{2,10},{3,11},{4,12},{5,13},{6,14},{7,15},{8,0},{9,1},... | collective-permute-start | bytes 393224 | tf_op jit(solution)/shard_map/ppermute | solution.py:357
  33.6 0.2 shard_map.73.refs_6_
  33.8 0.3 shard_map.74.a
  34.2 6.4 %collective-permute-done.8 = f32[128,256]{1,0:T(8,128)S(1)} collective-permute-done((f32[128,256]{1,0:T(8,128)S(1)}, f32[128,256]{1,0:T(8,128)S(1)}, u32[]{:S(2)}, u32[]{:S(2)}) %collective-permute-start.8) | collective-permute-done | bytes 131104 | tf_op jit(solution)/shard_map/ppermute | solution.py:357
  40.6 1.6 %collective-permute-start.10 = (f32[128,256]{1,0:T(8,128)S(1)}, f32[128,256]{1,0:T(8,128)S(1)}, u32[]{:S(2)}, u32[]{:S(2)}) collective-permute-start(f32[128,256]{1,0:T(8,128)S(1)} %slice_add_fusion.1.own), channel_id=1, source_target_pairs={{0,2},{1,3},{2,0},{3,1},{4,6},{5,7},{6,4},{7,5},{8,10},{9,11},{10,... | collective-permute-start | bytes 393224 | tf_op jit(solution)/shard_map/ppermute | solution.py:357
  42.3 2.9 %collective-permute-start.12 = (f32[64,256]{1,0:T(8,128)S(1)}, f32[64,256]{1,0:T(8,128)S(1)}, u32[]{:S(2)}, u32[]{:S(2)}) collective-permute-start(f32[64,256]{1,0:T(8,128)S(1)} %slice_add_fusion.4), channel_id=1, source_target_pairs={{0,8},{1,9},{2,10},{3,11},{4,12},{5,13},{6,14},{7,15},{8,0},{9,1},... | collective-permute-start | bytes 196616 | tf_op jit(solution)/shard_map/ppermute | solution.py:357
  45.2 3.4 %collective-permute-done.13 = f32[64,256]{1,0:T(8,128)S(1)} collective-permute-done((f32[64,256]{1,0:T(8,128)S(1)}, f32[64,256]{1,0:T(8,128)S(1)}, u32[]{:S(2)}, u32[]{:S(2)}) %collective-permute-start.13) | collective-permute-done | bytes 65568 | tf_op jit(solution)/shard_map/ppermute | solution.py:357
  48.7 0.8 %collective-permute-start.15 = (f32[64,256]{1,0:T(8,128)S(1)}, f32[64,256]{1,0:T(8,128)S(1)}, u32[]{:S(2)}, u32[]{:S(2)}) collective-permute-start(f32[64,256]{1,0:T(8,128)S(1)} %add.23.refs_5_), channel_id=1, source_target_pairs={{0,4},{1,5},{2,6},{3,7},{4,0},{5,1},{6,2},{7,3},{8,12},{9,13},{10,... | collective-permute-start | bytes 196616 | tf_op jit(solution)/shard_map/ppermute | solution.py:357
  49.5 0.5 collective-permute-start.11
  50.0 0.1 collective-permute-done.12
  50.1 1.6 %collective-permute-start.14 = (f32[64,256]{1,0:T(8,128)S(1)}, f32[64,256]{1,0:T(8,128)S(1)}, u32[]{:S(2)}, u32[]{:S(2)}) collective-permute-start(f32[64,256]{1,0:T(8,128)S(1)} %slice_add_fusion.3.refs_4_), channel_id=1, source_target_pairs={{0,4},{1,5},{2,6},{3,7},{4,0},{5,1},{6,2},{7,3},{8,12},{9,13},{10,... | collective-permute-start | bytes 196616 | tf_op jit(solution)/shard_map/ppermute | solution.py:357
  53.0 0.1 shard_map.81
  53.1 0.2 collective-permute-done.15.refs_7_
  53.3 1.1 %collective-permute-done.14.refs_6_ = f32[64,256]{1,0:T(8,128)S(1)} collective-permute-done((f32[64,256]{1,0:T(8,128)S(1)}, f32[64,256]{1,0:T(8,128)S(1)}, u32[]{:S(2)}, u32[]{:S(2)}) %collective-permute-start.14) | collective-permute-done | bytes 65568 | tf_op jit(solution)/shard_map/ppermute | solution.py:357
  54.4 1.3 %score.1 = bf16[512,256]{1,0:T(8,128)(2,1)} custom-call(f32[1]{0:T(128)S(6)} %copy.8.scale, f32[1]{0:T(128)S(6)} %copy.9.bias, bf16[128,512]{1,0:T(8,128)(2,1)S(1)} %get-tuple-element.30.refs_0_, bf16[128,512]{1,0:T(8,128)(2,1)S(1)} %get-tuple-element.31.refs_1_, f32[128,256]{1,0:T(8,128)S(1)} %collective-permute-done.10.refs_2_, ...), custom_call_target="tpu_custom_call" | custom-call | tf_op jit(solution)/shard_map/score/pallas_call | solution.py:332
  (17 shorter events, 0.3 us)
Async XLA Ops:
  8.7 6.7 %collective-permute-start = (f32[136,256]{1,0:T(8,128)S(1)}, f32[136,256]{1,0:T(8,128)S(1)}, u32[]{:S(2)}, u32[]{:S(2)}) collective-permute-start(f32[136,256]{1,0:T(8,128)S(1)} %get-tuple-element.19), channel_id=1, source_target_pairs={{0,2},{1,3},{2,0},{3,1},{4,6},{5,7},{6,4},{7,5},{8,10},{9,11},{10,... | collective-permute-start | bytes 417800 | tf_op jit(solution)/shard_map/ppermute | solution.py:357
  11.8 6.5 %collective-permute-start.1 = (f32[136,256]{1,0:T(8,128)S(1)}, f32[136,256]{1,0:T(8,128)S(1)}, u32[]{:S(2)}, u32[]{:S(2)}) collective-permute-start(f32[136,256]{1,0:T(8,128)S(1)} %get-tuple-element.20), channel_id=1, source_target_pairs={{0,4},{1,5},{2,6},{3,7},{4,0},{5,1},{6,2},{7,3},{8,12},{9,13},{10,... | collective-permute-start | bytes 417800 | tf_op jit(solution)/shard_map/ppermute | solution.py:357
  13.3 6.3 %collective-permute-start.2 = (f32[136,256]{1,0:T(8,128)S(1)}, f32[136,256]{1,0:T(8,128)S(1)}, u32[]{:S(2)}, u32[]{:S(2)}) collective-permute-start(f32[136,256]{1,0:T(8,128)S(1)} %get-tuple-element.21), channel_id=1, source_target_pairs={{0,6},{1,7},{2,4},{3,5},{4,2},{5,3},{6,0},{7,1},{8,14},{9,15},{10,... | collective-permute-start | bytes 417800 | tf_op jit(solution)/shard_map/ppermute | solution.py:357
  20.0 10.7 %collective-permute-start.7 = (f32[192,256]{1,0:T(8,128)S(1)}, f32[192,256]{1,0:T(8,128)S(1)}, u32[]{:S(2)}, u32[]{:S(2)}) collective-permute-start(f32[192,256]{1,0:T(8,128)S(1)} %shard_map.80), channel_id=1, source_target_pairs={{0,1},{1,0},{2,3},{3,2},{4,5},{5,4},{6,7},{7,6},{8,9},{9,8},{10,11... | collective-permute-start | bytes 589832 | tf_op jit(solution)/shard_map/ppermute | solution.py:357
  20.1 5.9 %collective-permute-start.3 = (f32[128,256]{1,0:T(8,128)S(1)}, f32[128,256]{1,0:T(8,128)S(1)}, u32[]{:S(2)}, u32[]{:S(2)}) collective-permute-start(f32[128,256]{1,0:T(8,128)S(1)} %get-tuple-element.22), channel_id=1, source_target_pairs={{0,2},{1,3},{2,0},{3,1},{4,6},{5,7},{6,4},{7,5},{8,10},{9,11},{10,... | collective-permute-start | bytes 393224 | tf_op jit(solution)/shard_map/ppermute | solution.py:357
  21.8 6.4 %collective-permute-start.4 = (f32[128,256]{1,0:T(8,128)S(1)}, f32[128,256]{1,0:T(8,128)S(1)}, u32[]{:S(2)}, u32[]{:S(2)}) collective-permute-start(f32[128,256]{1,0:T(8,128)S(1)} %get-tuple-element.23), channel_id=1, source_target_pairs={{0,4},{1,5},{2,6},{3,7},{4,0},{5,1},{6,2},{7,3},{8,12},{9,13},{10,... | collective-permute-start | bytes 393224 | tf_op jit(solution)/shard_map/ppermute | solution.py:357
  23.4 6.6 %collective-permute-start.5 = (f32[128,256]{1,0:T(8,128)S(1)}, f32[128,256]{1,0:T(8,128)S(1)}, u32[]{:S(2)}, u32[]{:S(2)}) collective-permute-start(f32[128,256]{1,0:T(8,128)S(1)} %get-tuple-element.24), channel_id=1, source_target_pairs={{0,6},{1,7},{2,4},{3,5},{4,2},{5,3},{6,0},{7,1},{8,14},{9,15},{10,... | collective-permute-start | bytes 393224 | tf_op jit(solution)/shard_map/ppermute | solution.py:357
  30.3 3.8 %collective-permute-start.6 = (f32[192,256]{1,0:T(8,128)S(1)}, f32[192,256]{1,0:T(8,128)S(1)}, u32[]{:S(2)}, u32[]{:S(2)}) collective-permute-start(f32[192,256]{1,0:T(8,128)S(1)} %shard_map.76), channel_id=1, source_target_pairs={{0,1},{1,0},{2,3},{3,2},{4,5},{5,4},{6,7},{7,6},{8,9},{9,8},{10,11... | collective-permute-start | bytes 589832 | tf_op jit(solution)/shard_map/ppermute | solution.py:357
  30.8 9.8 %collective-permute-start.8 = (f32[128,256]{1,0:T(8,128)S(1)}, f32[128,256]{1,0:T(8,128)S(1)}, u32[]{:S(2)}, u32[]{:S(2)}) collective-permute-start(f32[128,256]{1,0:T(8,128)S(1)} %slice_add_fusion), channel_id=1, source_target_pairs={{0,8},{1,9},{2,10},{3,11},{4,12},{5,13},{6,14},{7,15},{8,0},{9,1},... | collective-permute-start | bytes 393224 | tf_op jit(solution)/shard_map/ppermute | solution.py:357
  40.6 8.9 %collective-permute-start.10 = (f32[128,256]{1,0:T(8,128)S(1)}, f32[128,256]{1,0:T(8,128)S(1)}, u32[]{:S(2)}, u32[]{:S(2)}) collective-permute-start(f32[128,256]{1,0:T(8,128)S(1)} %slice_add_fusion.1.own), channel_id=1, source_target_pairs={{0,2},{1,3},{2,0},{3,1},{4,6},{5,7},{6,4},{7,5},{8,10},{9,11},{10,... | collective-permute-start | bytes 393224 | tf_op jit(solution)/shard_map/ppermute | solution.py:357
  42.2 6.4 %collective-permute-start.13 = (f32[64,256]{1,0:T(8,128)S(1)}, f32[64,256]{1,0:T(8,128)S(1)}, u32[]{:S(2)}, u32[]{:S(2)}) collective-permute-start(f32[64,256]{1,0:T(8,128)S(1)} %slice_add_fusion.2), channel_id=1, source_target_pairs={{0,8},{1,9},{2,10},{3,11},{4,12},{5,13},{6,14},{7,15},{8,0},{9,1},... | collective-permute-start | bytes 196616 | tf_op jit(solution)/shard_map/ppermute | solution.py:357
  42.3 7.8 %collective-permute-start.12 = (f32[64,256]{1,0:T(8,128)S(1)}, f32[64,256]{1,0:T(8,128)S(1)}, u32[]{:S(2)}, u32[]{:S(2)}) collective-permute-start(f32[64,256]{1,0:T(8,128)S(1)} %slice_add_fusion.4), channel_id=1, source_target_pairs={{0,8},{1,9},{2,10},{3,11},{4,12},{5,13},{6,14},{7,15},{8,0},{9,1},... | collective-permute-start | bytes 196616 | tf_op jit(solution)/shard_map/ppermute | solution.py:357
  48.7 4.7 %collective-permute-start.15 = (f32[64,256]{1,0:T(8,128)S(1)}, f32[64,256]{1,0:T(8,128)S(1)}, u32[]{:S(2)}, u32[]{:S(2)}) collective-permute-start(f32[64,256]{1,0:T(8,128)S(1)} %add.23.refs_5_), channel_id=1, source_target_pairs={{0,4},{1,5},{2,6},{3,7},{4,0},{5,1},{6,2},{7,3},{8,12},{9,13},{10,... | collective-permute-start | bytes 196616 | tf_op jit(solution)/shard_map/ppermute | solution.py:357
  49.5 3.5 %collective-permute-start.9 = (f32[128,256]{1,0:T(8,128)S(1)}, f32[128,256]{1,0:T(8,128)S(1)}, u32[]{:S(2)}, u32[]{:S(2)}) collective-permute-start(f32[128,256]{1,0:T(8,128)S(1)} %slice_add_fusion.1.own), channel_id=1, source_target_pairs={{0,1},{1,0},{2,3},{3,2},{4,5},{5,4},{6,7},{7,6},{8,9},{9,8},{10,11... | collective-permute-start | bytes 393224 | tf_op jit(solution)/shard_map/ppermute | solution.py:357
  49.5 4.9 %collective-permute-start.11 = (f32[128,256]{1,0:T(8,128)S(1)}, f32[128,256]{1,0:T(8,128)S(1)}, u32[]{:S(2)}, u32[]{:S(2)}) collective-permute-start(f32[128,256]{1,0:T(8,128)S(1)} %collective-permute-done.10.refs_2_), channel_id=1, source_target_pairs={{0,1},{1,0},{2,3},{3,2},{4,5},{5,4},{6,7},{7,6},{8,9},{9,8},{10,11... | collective-permute-start | bytes 393224 | tf_op jit(solution)/shard_map/ppermute | solution.py:357
  50.1 4.3 %collective-permute-start.14 = (f32[64,256]{1,0:T(8,128)S(1)}, f32[64,256]{1,0:T(8,128)S(1)}, u32[]{:S(2)}, u32[]{:S(2)}) collective-permute-start(f32[64,256]{1,0:T(8,128)S(1)} %slice_add_fusion.3.refs_4_), channel_id=1, source_target_pairs={{0,4},{1,5},{2,6},{3,7},{4,0},{5,1},{6,2},{7,3},{8,12},{9,13},{10,... | collective-permute-start | bytes 196616 | tf_op jit(solution)/shard_map/ppermute | solution.py:357
where the time goes:
time: 55.8 us; the launch traced here: 55.7 us
  waiting for transfers between devices  23.4 us (42%)
  starting transfers between devices  18.6 us (33%)
  Pallas kernels  12.1 us (22%)
  between operations  1.47 us (3%)
    ppermute x16, waiting for transfers between devices, flip(): return lax.ppermute(value, ('enrol', 'probe'), pairs)  23.4 us
    ppermute x16, starting transfers between devices, flip(): return lax.ppermute(value, ('enrol', 'probe'), pairs)  18.6 us
    pallas_call x1, Pallas kernels, embed(): pl.pallas_call(functools.partial(embed_kernel, n_enrol, n_probe), out_sha...  8.73 us
    pallas_call x9, Pallas kernels, local(): pl.pallas_call(kernel, out_shape=[jax.ShapeDtypeStruct(shape, kind) for s...  2.11 us
    pallas_call x1, Pallas kernels, score(): pl.pallas_call(functools.partial(score_kernel, n_enrol, n_probe), out_sha...  1.28 us
  transfers between devices with their start and end apart: 16, of which 11 were waited for; matrix products, arithmetic and copies ran while one was open for 0% of the time, Pallas kernels for 3%

commit v1 on v0

--- a/solution.py
+++ b/solution.py
@@ -321,8 +321,10 @@
         else:
             high, low = split(unit(enrol[k][...]))
         put(e3, p ^ k, ET_OWN, (high, low, high))
-    cosine = dot(e3[...], p3[...], ((1,), (1,)))
-    out[...] = jax.nn.sigmoid(scale[0] * cosine + bias[0]).astype(BF16)
+    for start in range(0, e3.shape[0], 2 * ET_OWN):
+        at = pl.ds(start, 2 * ET_OWN)
+        cosine = dot(e3[at, :], p3[...], ((1,), (1,)))
+        out[at, :] = jax.nn.sigmoid(scale[0] * cosine + bias[0]).astype(BF16)
 
 
 def score(n_enrol, n_probe, scale, bias, enrol, probe):

time: 55.8 us -> 55.9 us (level)
  no operation moved by 1% of the time
where the time goes in v1:
time: 55.9 us; the launch traced here: 55.7 us
  waiting for transfers between devices  23.4 us (42%)
  starting transfers between devices  18.6 us (33%)
  Pallas kernels  12.1 us (22%)
  between operations  1.47 us (3%)
    ppermute x16, waiting for transfers between devices, flip(): return lax.ppermute(value, ('enrol', 'probe'), pairs)  23.4 us
    ppermute x16, starting transfers between devices, flip(): return lax.ppermute(value, ('enrol', 'probe'), pairs)  18.6 us
    pallas_call x1, Pallas kernels, embed(): pl.pallas_call(functools.partial(embed_kernel, n_enrol, n_probe), out_sha...  8.73 us
    pallas_call x9, Pallas kernels, local(): pl.pallas_call(kernel, out_shape=[jax.ShapeDtypeStruct(shape, kind) for s...  2.11 us
    pallas_call x1, Pallas kernels, score(): pl.pallas_call(functools.partial(score_kernel, n_enrol, n_probe), out_sha...  1.29 us
  transfers between devices with their start and end apart: 16, of which 11 were waited for; matrix products, arithmetic and copies ran while one was open for 0% of the time, Pallas kernels for 3%

profile of v1, /device:TPU:0, one launch (start us, length us, event | category | flops | bytes accessed | tf_op | source)
XLA Modules:
  0.0 55.7 jit_solution(14360186298427071275)
XLA Ops:
  0.0 8.7 %embed.1 = (f32[136,256]{1,0:T(8,128)S(1)}, f32[136,256]{1,0:T(8,128)S(1)}, f32[136,256]{1,0:T(8,128)S(1)}, f32[136,256]{1,0:T(8,128)S(1)}, f32[128,256]{1,0:T(8...) custom-call(s32[1,16]{1,0:T(1,128)} %count_hbm.1, s32[4,128]{1,0:T(4,128)} %bitcast.1, ...), custom_call_target="tpu_custom_call" | custom-call | tf_op jit(solution)/shard_map/embed/pallas_call | solution.py:219
  8.7 3.0 %collective-permute-start = (f32[136,256]{1,0:T(8,128)S(1)}, f32[136,256]{1,0:T(8,128)S(1)}, u32[]{:S(2)}, u32[]{:S(2)}) collective-permute-start(f32[136,256]{1,0:T(8,128)S(1)} %get-tuple-element.19), channel_id=1, source_target_pairs={{0,2},{1,3},{2,0},{3,1},{4,6},{5,7},{6,4},{7,5},{8,10},{9,11},{10,... | collective-permute-start | bytes 417800 | tf_op jit(solution)/shard_map/ppermute | solution.py:359
  11.8 1.6 %collective-permute-start.1 = (f32[136,256]{1,0:T(8,128)S(1)}, f32[136,256]{1,0:T(8,128)S(1)}, u32[]{:S(2)}, u32[]{:S(2)}) collective-permute-start(f32[136,256]{1,0:T(8,128)S(1)} %get-tuple-element.20), channel_id=1, source_target_pairs={{0,4},{1,5},{2,6},{3,7},{4,0},{5,1},{6,2},{7,3},{8,12},{9,13},{10,... | collective-permute-start | bytes 417800 | tf_op jit(solution)/shard_map/ppermute | solution.py:359
  13.4 0.2 shard_map.78
  13.6 1.8 %collective-permute-done.refs_0_ = f32[136,256]{1,0:T(8,128)S(1)} collective-permute-done((f32[136,256]{1,0:T(8,128)S(1)}, f32[136,256]{1,0:T(8,128)S(1)}, u32[]{:S(2)}, u32[]{:S(2)}) %collective-permute-start) | collective-permute-done | bytes 139296 | tf_op jit(solution)/shard_map/ppermute | solution.py:359
  15.4 2.9 %collective-permute-done.1.refs_1_ = f32[136,256]{1,0:T(8,128)S(1)} collective-permute-done((f32[136,256]{1,0:T(8,128)S(1)}, f32[136,256]{1,0:T(8,128)S(1)}, u32[]{:S(2)}, u32[]{:S(2)}) %collective-permute-start.1) | collective-permute-done | bytes 139296 | tf_op jit(solution)/shard_map/ppermute | solution.py:359
  18.3 1.4 %collective-permute-done.2.refs_2_ = f32[136,256]{1,0:T(8,128)S(1)} collective-permute-done((f32[136,256]{1,0:T(8,128)S(1)}, f32[136,256]{1,0:T(8,128)S(1)}, u32[]{:S(2)}, u32[]{:S(2)}) %collective-permute-start.2) | collective-permute-done | bytes 139296 | tf_op jit(solution)/shard_map/ppermute | solution.py:359
  19.7 0.3 shard_map.80
  20.1 1.7 %collective-permute-start.3 = (f32[128,256]{1,0:T(8,128)S(1)}, f32[128,256]{1,0:T(8,128)S(1)}, u32[]{:S(2)}, u32[]{:S(2)}) collective-permute-start(f32[128,256]{1,0:T(8,128)S(1)} %get-tuple-element.22), channel_id=1, source_target_pairs={{0,2},{1,3},{2,0},{3,1},{4,6},{5,7},{6,4},{7,5},{8,10},{9,11},{10,... | collective-permute-start | bytes 393224 | tf_op jit(solution)/shard_map/ppermute | solution.py:359
  21.8 1.6 %collective-permute-start.4 = (f32[128,256]{1,0:T(8,128)S(1)}, f32[128,256]{1,0:T(8,128)S(1)}, u32[]{:S(2)}, u32[]{:S(2)}) collective-permute-start(f32[128,256]{1,0:T(8,128)S(1)} %get-tuple-element.23), channel_id=1, source_target_pairs={{0,4},{1,5},{2,6},{3,7},{4,0},{5,1},{6,2},{7,3},{8,12},{9,13},{10,... | collective-permute-start | bytes 393224 | tf_op jit(solution)/shard_map/ppermute | solution.py:359
  23.4 0.3 collective-permute-start.5
  23.7 0.2 shard_map.75.refs_6_
  23.9 2.1 %collective-permute-done.3.refs_3_ = f32[128,256]{1,0:T(8,128)S(1)} collective-permute-done((f32[128,256]{1,0:T(8,128)S(1)}, f32[128,256]{1,0:T(8,128)S(1)}, u32[]{:S(2)}, u32[]{:S(2)}) %collective-permute-start.3) | collective-permute-done | bytes 131104 | tf_op jit(solution)/shard_map/ppermute | solution.py:359
  26.0 2.2 %collective-permute-done.4.refs_4_ = f32[128,256]{1,0:T(8,128)S(1)} collective-permute-done((f32[128,256]{1,0:T(8,128)S(1)}, f32[128,256]{1,0:T(8,128)S(1)}, u32[]{:S(2)}, u32[]{:S(2)}) %collective-permute-start.4) | collective-permute-done | bytes 131104 | tf_op jit(solution)/shard_map/ppermute | solution.py:359
  28.2 1.8 %collective-permute-done.5.refs_5_ = f32[128,256]{1,0:T(8,128)S(1)} collective-permute-done((f32[128,256]{1,0:T(8,128)S(1)}, f32[128,256]{1,0:T(8,128)S(1)}, u32[]{:S(2)}, u32[]{:S(2)}) %collective-permute-start.5) | collective-permute-done | bytes 131104 | tf_op jit(solution)/shard_map/ppermute | solution.py:359
  30.0 0.3 shard_map.76
  30.4 0.3 shard_map.79
  30.8 2.8 %collective-permute-start.8 = (f32[128,256]{1,0:T(8,128)S(1)}, f32[128,256]{1,0:T(8,128)S(1)}, u32[]{:S(2)}, u32[]{:S(2)}) collective-permute-start(f32[128,256]{1,0:T(8,128)S(1)} %slice_add_fusion), channel_id=1, source_target_pairs={{0,8},{1,9},{2,10},{3,11},{4,12},{5,13},{6,14},{7,15},{8,0},{9,1},... | collective-permute-start | bytes 393224 | tf_op jit(solution)/shard_map/ppermute | solution.py:359
  33.6 0.2 shard_map.73.refs_6_
  33.8 0.3 shard_map.74.a
  34.2 6.4 %collective-permute-done.8 = f32[128,256]{1,0:T(8,128)S(1)} collective-permute-done((f32[128,256]{1,0:T(8,128)S(1)}, f32[128,256]{1,0:T(8,128)S(1)}, u32[]{:S(2)}, u32[]{:S(2)}) %collective-permute-start.8) | collective-permute-done | bytes 131104 | tf_op jit(solution)/shard_map/ppermute | solution.py:359
  40.6 1.6 %collective-permute-start.10 = (f32[128,256]{1,0:T(8,128)S(1)}, f32[128,256]{1,0:T(8,128)S(1)}, u32[]{:S(2)}, u32[]{:S(2)}) collective-permute-start(f32[128,256]{1,0:T(8,128)S(1)} %slice_add_fusion.1.own), channel_id=1, source_target_pairs={{0,2},{1,3},{2,0},{3,1},{4,6},{5,7},{6,4},{7,5},{8,10},{9,11},{10,... | collective-permute-start | bytes 393224 | tf_op jit(solution)/shard_map/ppermute | solution.py:359
  42.3 2.9 %collective-permute-start.12 = (f32[64,256]{1,0:T(8,128)S(1)}, f32[64,256]{1,0:T(8,128)S(1)}, u32[]{:S(2)}, u32[]{:S(2)}) collective-permute-start(f32[64,256]{1,0:T(8,128)S(1)} %slice_add_fusion.4), channel_id=1, source_target_pairs={{0,8},{1,9},{2,10},{3,11},{4,12},{5,13},{6,14},{7,15},{8,0},{9,1},... | collective-permute-start | bytes 196616 | tf_op jit(solution)/shard_map/ppermute | solution.py:359
  45.2 3.4 %collective-permute-done.13 = f32[64,256]{1,0:T(8,128)S(1)} collective-permute-done((f32[64,256]{1,0:T(8,128)S(1)}, f32[64,256]{1,0:T(8,128)S(1)}, u32[]{:S(2)}, u32[]{:S(2)}) %collective-permute-start.13) | collective-permute-done | bytes 65568 | tf_op jit(solution)/shard_map/ppermute | solution.py:359
  48.7 0.8 %collective-permute-start.15 = (f32[64,256]{1,0:T(8,128)S(1)}, f32[64,256]{1,0:T(8,128)S(1)}, u32[]{:S(2)}, u32[]{:S(2)}) collective-permute-start(f32[64,256]{1,0:T(8,128)S(1)} %add.23.refs_5_), channel_id=1, source_target_pairs={{0,4},{1,5},{2,6},{3,7},{4,0},{5,1},{6,2},{7,3},{8,12},{9,13},{10,... | collective-permute-start | bytes 196616 | tf_op jit(solution)/shard_map/ppermute | solution.py:359
  49.5 0.5 collective-permute-start.11
  50.0 0.1 collective-permute-done.12
  50.1 1.6 %collective-permute-start.14 = (f32[64,256]{1,0:T(8,128)S(1)}, f32[64,256]{1,0:T(8,128)S(1)}, u32[]{:S(2)}, u32[]{:S(2)}) collective-permute-start(f32[64,256]{1,0:T(8,128)S(1)} %slice_add_fusion.3.refs_4_), channel_id=1, source_target_pairs={{0,4},{1,5},{2,6},{3,7},{4,0},{5,1},{6,2},{7,3},{8,12},{9,13},{10,... | collective-permute-start | bytes 196616 | tf_op jit(solution)/shard_map/ppermute | solution.py:359
  53.0 0.1 shard_map.81
  53.1 0.2 collective-permute-done.15.refs_7_
  53.3 1.1 %collective-permute-done.14.refs_6_ = f32[64,256]{1,0:T(8,128)S(1)} collective-permute-done((f32[64,256]{1,0:T(8,128)S(1)}, f32[64,256]{1,0:T(8,128)S(1)}, u32[]{:S(2)}, u32[]{:S(2)}) %collective-permute-start.14) | collective-permute-done | bytes 65568 | tf_op jit(solution)/shard_map/ppermute | solution.py:359
  54.4 1.3 %score.1 = bf16[512,256]{1,0:T(8,128)(2,1)} custom-call(f32[1]{0:T(128)S(6)} %copy.8.scale, f32[1]{0:T(128)S(6)} %copy.9.bias, bf16[128,512]{1,0:T(8,128)(2,1)S(1)} %get-tuple-element.30.refs_0_, bf16[128,512]{1,0:T(8,128)(2,1)S(1)} %get-tuple-element.31.refs_1_, f32[128,256]{1,0:T(8,128)S(1)} %collective-permute-done.10.refs_2_, ...), custom_call_target="tpu_custom_call" | custom-call | tf_op jit(solution)/shard_map/score/pallas_call | solution.py:334
  (17 shorter events, 0.3 us)
Async XLA Ops:
  8.7 6.7 %collective-permute-start = (f32[136,256]{1,0:T(8,128)S(1)}, f32[136,256]{1,0:T(8,128)S(1)}, u32[]{:S(2)}, u32[]{:S(2)}) collective-permute-start(f32[136,256]{1,0:T(8,128)S(1)} %get-tuple-element.19), channel_id=1, source_target_pairs={{0,2},{1,3},{2,0},{3,1},{4,6},{5,7},{6,4},{7,5},{8,10},{9,11},{10,... | collective-permute-start | bytes 417800 | tf_op jit(solution)/shard_map/ppermute | solution.py:359
  11.8 6.5 %collective-permute-start.1 = (f32[136,256]{1,0:T(8,128)S(1)}, f32[136,256]{1,0:T(8,128)S(1)}, u32[]{:S(2)}, u32[]{:S(2)}) collective-permute-start(f32[136,256]{1,0:T(8,128)S(1)} %get-tuple-element.20), channel_id=1, source_target_pairs={{0,4},{1,5},{2,6},{3,7},{4,0},{5,1},{6,2},{7,3},{8,12},{9,13},{10,... | collective-permute-start | bytes 417800 | tf_op jit(solution)/shard_map/ppermute | solution.py:359
  13.3 6.3 %collective-permute-start.2 = (f32[136,256]{1,0:T(8,128)S(1)}, f32[136,256]{1,0:T(8,128)S(1)}, u32[]{:S(2)}, u32[]{:S(2)}) collective-permute-start(f32[136,256]{1,0:T(8,128)S(1)} %get-tuple-element.21), channel_id=1, source_target_pairs={{0,6},{1,7},{2,4},{3,5},{4,2},{5,3},{6,0},{7,1},{8,14},{9,15},{10,... | collective-permute-start | bytes 417800 | tf_op jit(solution)/shard_map/ppermute | solution.py:359
  20.0 10.7 %collective-permute-start.7 = (f32[192,256]{1,0:T(8,128)S(1)}, f32[192,256]{1,0:T(8,128)S(1)}, u32[]{:S(2)}, u32[]{:S(2)}) collective-permute-start(f32[192,256]{1,0:T(8,128)S(1)} %shard_map.80), channel_id=1, source_target_pairs={{0,1},{1,0},{2,3},{3,2},{4,5},{5,4},{6,7},{7,6},{8,9},{9,8},{10,11... | collective-permute-start | bytes 589832 | tf_op jit(solution)/shard_map/ppermute | solution.py:359
  20.1 5.9 %collective-permute-start.3 = (f32[128,256]{1,0:T(8,128)S(1)}, f32[128,256]{1,0:T(8,128)S(1)}, u32[]{:S(2)}, u32[]{:S(2)}) collective-permute-start(f32[128,256]{1,0:T(8,128)S(1)} %get-tuple-element.22), channel_id=1, source_target_pairs={{0,2},{1,3},{2,0},{3,1},{4,6},{5,7},{6,4},{7,5},{8,10},{9,11},{10,... | collective-permute-start | bytes 393224 | tf_op jit(solution)/shard_map/ppermute | solution.py:359
  21.8 6.4 %collective-permute-start.4 = (f32[128,256]{1,0:T(8,128)S(1)}, f32[128,256]{1,0:T(8,128)S(1)}, u32[]{:S(2)}, u32[]{:S(2)}) collective-permute-start(f32[128,256]{1,0:T(8,128)S(1)} %get-tuple-element.23), channel_id=1, source_target_pairs={{0,4},{1,5},{2,6},{3,7},{4,0},{5,1},{6,2},{7,3},{8,12},{9,13},{10,... | collective-permute-start | bytes 393224 | tf_op jit(solution)/shard_map/ppermute | solution.py:359
  23.4 6.6 %collective-permute-start.5 = (f32[128,256]{1,0:T(8,128)S(1)}, f32[128,256]{1,0:T(8,128)S(1)}, u32[]{:S(2)}, u32[]{:S(2)}) collective-permute-start(f32[128,256]{1,0:T(8,128)S(1)} %get-tuple-element.24), channel_id=1, source_target_pairs={{0,6},{1,7},{2,4},{3,5},{4,2},{5,3},{6,0},{7,1},{8,14},{9,15},{10,... | collective-permute-start | bytes 393224 | tf_op jit(solution)/shard_map/ppermute | solution.py:359
  30.3 3.8 %collective-permute-start.6 = (f32[192,256]{1,0:T(8,128)S(1)}, f32[192,256]{1,0:T(8,128)S(1)}, u32[]{:S(2)}, u32[]{:S(2)}) collective-permute-start(f32[192,256]{1,0:T(8,128)S(1)} %shard_map.76), channel_id=1, source_target_pairs={{0,1},{1,0},{2,3},{3,2},{4,5},{5,4},{6,7},{7,6},{8,9},{9,8},{10,11... | collective-permute-start | bytes 589832 | tf_op jit(solution)/shard_map/ppermute | solution.py:359
  30.8 9.8 %collective-permute-start.8 = (f32[128,256]{1,0:T(8,128)S(1)}, f32[128,256]{1,0:T(8,128)S(1)}, u32[]{:S(2)}, u32[]{:S(2)}) collective-permute-start(f32[128,256]{1,0:T(8,128)S(1)} %slice_add_fusion), channel_id=1, source_target_pairs={{0,8},{1,9},{2,10},{3,11},{4,12},{5,13},{6,14},{7,15},{8,0},{9,1},... | collective-permute-start | bytes 393224 | tf_op jit(solution)/shard_map/ppermute | solution.py:359
  40.6 8.9 %collective-permute-start.10 = (f32[128,256]{1,0:T(8,128)S(1)}, f32[128,256]{1,0:T(8,128)S(1)}, u32[]{:S(2)}, u32[]{:S(2)}) collective-permute-start(f32[128,256]{1,0:T(8,128)S(1)} %slice_add_fusion.1.own), channel_id=1, source_target_pairs={{0,2},{1,3},{2,0},{3,1},{4,6},{5,7},{6,4},{7,5},{8,10},{9,11},{10,... | collective-permute-start | bytes 393224 | tf_op jit(solution)/shard_map/ppermute | solution.py:359
  42.2 6.4 %collective-permute-start.13 = (f32[64,256]{1,0:T(8,128)S(1)}, f32[64,256]{1,0:T(8,128)S(1)}, u32[]{:S(2)}, u32[]{:S(2)}) collective-permute-start(f32[64,256]{1,0:T(8,128)S(1)} %slice_add_fusion.2), channel_id=1, source_target_pairs={{0,8},{1,9},{2,10},{3,11},{4,12},{5,13},{6,14},{7,15},{8,0},{9,1},... | collective-permute-start | bytes 196616 | tf_op jit(solution)/shard_map/ppermute | solution.py:359
  42.3 7.8 %collective-permute-start.12 = (f32[64,256]{1,0:T(8,128)S(1)}, f32[64,256]{1,0:T(8,128)S(1)}, u32[]{:S(2)}, u32[]{:S(2)}) collective-permute-start(f32[64,256]{1,0:T(8,128)S(1)} %slice_add_fusion.4), channel_id=1, source_target_pairs={{0,8},{1,9},{2,10},{3,11},{4,12},{5,13},{6,14},{7,15},{8,0},{9,1},... | collective-permute-start | bytes 196616 | tf_op jit(solution)/shard_map/ppermute | solution.py:359
  48.7 4.7 %collective-permute-start.15 = (f32[64,256]{1,0:T(8,128)S(1)}, f32[64,256]{1,0:T(8,128)S(1)}, u32[]{:S(2)}, u32[]{:S(2)}) collective-permute-start(f32[64,256]{1,0:T(8,128)S(1)} %add.23.refs_5_), channel_id=1, source_target_pairs={{0,4},{1,5},{2,6},{3,7},{4,0},{5,1},{6,2},{7,3},{8,12},{9,13},{10,... | collective-permute-start | bytes 196616 | tf_op jit(solution)/shard_map/ppermute | solution.py:359
  49.5 3.5 %collective-permute-start.9 = (f32[128,256]{1,0:T(8,128)S(1)}, f32[128,256]{1,0:T(8,128)S(1)}, u32[]{:S(2)}, u32[]{:S(2)}) collective-permute-start(f32[128,256]{1,0:T(8,128)S(1)} %slice_add_fusion.1.own), channel_id=1, source_target_pairs={{0,1},{1,0},{2,3},{3,2},{4,5},{5,4},{6,7},{7,6},{8,9},{9,8},{10,11... | collective-permute-start | bytes 393224 | tf_op jit(solution)/shard_map/ppermute | solution.py:359
  49.5 4.9 %collective-permute-start.11 = (f32[128,256]{1,0:T(8,128)S(1)}, f32[128,256]{1,0:T(8,128)S(1)}, u32[]{:S(2)}, u32[]{:S(2)}) collective-permute-start(f32[128,256]{1,0:T(8,128)S(1)} %collective-permute-done.10.refs_2_), channel_id=1, source_target_pairs={{0,1},{1,0},{2,3},{3,2},{4,5},{5,4},{6,7},{7,6},{8,9},{9,8},{10,11... | collective-permute-start | bytes 393224 | tf_op jit(solution)/shard_map/ppermute | solution.py:359
  50.1 4.3 %collective-permute-start.14 = (f32[64,256]{1,0:T(8,128)S(1)}, f32[64,256]{1,0:T(8,128)S(1)}, u32[]{:S(2)}, u32[]{:S(2)}) collective-permute-start(f32[64,256]{1,0:T(8,128)S(1)} %slice_add_fusion.3.refs_4_), channel_id=1, source_target_pairs={{0,4},{1,5},{2,6},{3,7},{4,0},{5,1},{6,2},{7,3},{8,12},{9,13},{10,... | collective-permute-start | bytes 196616 | tf_op jit(solution)/shard_map/ppermute | solution.py:359
